TPU v7x, 128 devices: a whole 4x4x4 slice. The times are simulated.
128 devices in a mesh: walk: 16 (over y_hi, z, core), band: 8 (over y_lo, x).
Axes of the slice: x: 4, y: 4 (y_hi: 2, y_lo: 2; y = y_hi * 2 + y_lo), z: 4, core: 2. Of those that a mesh axis runs over, the one named last changes fastest.
Arguments:
- positions: float32 [2, 49152], P(None, 'walk'), may hold values from 0 to 1
- coefficients: bfloat16 [2, 18432, 1024], P(None, 'walk', 'band')
- lattice: int32 [2, 18432], replicated, may hold values from -76 to 76
- spin_labels: int32 [49152], P('walk'), may hold values from 0 to 1
- occupied: int32 [2, 48], replicated, may hold values from 0 to 1023
- features: bfloat16 [49152, 256], P('walk'), may hold values from -6 to 6
- orbital_head: bfloat16 [256, 192], replicated, may hold values from -0.029907227 to 0.029907227
Outputs:
- gradient: float32 [256, 192], replicated
All inputs are finite; a program needn't handle non-finite values.
Results may differ from a plain program's by a relative error of at most 0.0003.
Values may be sent and summed in bfloat16 or wider, within the bound.
No kernel may reach another device: no remote copies, remote signals or barrier semaphores. Data moves between devices by JAX's collectives and lax.ppermute only.
A program may use at most 128 MiB of HBM per device.

v0:
```python
import jax
import jax.numpy as jnp
from jax import lax
from jax.sharding import PartitionSpec as P

E = 96
TWO_PI = 6.283185307179586


def orbital_block(pos_x, pos_y, lat_x, lat_y, right_cos, right_sin):
    phase_angle = TWO_PI * (pos_x[:, None] * lat_x[None, :] + pos_y[:, None] * lat_y[None, :])
    cosine = jnp.cos(phase_angle)
    sine_part = jnp.sin(phase_angle)
    first = jnp.dot(
        cosine, right_cos, precision=lax.Precision.HIGHEST, preferred_element_type=jnp.float32
    )
    second = jnp.dot(
        sine_part, right_sin, precision=lax.Precision.HIGHEST, preferred_element_type=jnp.float32
    )
    return first + second


def spin_columns(orbitals, spin_labels):
    orbital_count = orbitals.shape[1] // 4
    spin_up = (spin_labels == 0)[:, None]
    real_pick = jnp.where(
        spin_up, orbitals[:, :orbital_count], orbitals[:, orbital_count : 2 * orbital_count]
    )
    imag_pick = jnp.where(
        spin_up,
        orbitals[:, 2 * orbital_count : 3 * orbital_count],
        orbitals[:, 3 * orbital_count :],
    )
    return jnp.concatenate([real_pick, imag_pick], axis=1)


def fit_from_target(target, spin_labels, features, orbital_head, walkers):
    half_width = target.shape[1]
    spin_up = (spin_labels == 0)[:, None]
    net_all = jnp.dot(features, orbital_head, preferred_element_type=jnp.float32)
    net_value = jnp.where(spin_up, net_all[:, :half_width], net_all[:, half_width:])
    scaled = (net_value - target) / walkers
    blank_rows = jnp.zeros_like(scaled)
    spread_rows = jnp.concatenate(
        [jnp.where(spin_up, scaled, blank_rows), jnp.where(spin_up, blank_rows, scaled)], axis=1
    )
    return lax.dot_general(
        features.astype(jnp.float32),
        spread_rows,
        (((0,), (0,)), ((), ())),
        precision=lax.Precision.HIGHEST,
        preferred_element_type=jnp.float32,
    )


def fit_gradient(orbitals, spin_labels, features, orbital_head, walkers):
    target = spin_columns(orbitals, spin_labels)
    return fit_from_target(target, spin_labels, features, orbital_head, walkers)


def local(positions, coefficients, lattice, spin_labels, occupied, features, orbital_head):
    walk_count = lax.axis_size("walk")
    band_count = lax.axis_size("band")
    band_index = lax.axis_index("band")
    occ_flat = occupied.reshape(-1)
    wave_count = lattice.shape[1]
    gathered = lax.all_gather(coefficients, "walk", axis=1, tiled=True)
    band_panel = lax.all_to_all(gathered, "band", split_axis=1, concat_axis=2, tiled=True)
    picked = jnp.take(band_panel, occ_flat, axis=2)
    local_lattice = lax.dynamic_slice_in_dim(
        lattice, band_index * (wave_count // band_count), wave_count // band_count, 1
    )
    right_cos = jnp.concatenate([picked[0], picked[1]], axis=1).astype(jnp.float32)
    right_sin = jnp.concatenate([-picked[1], picked[0]], axis=1).astype(jnp.float32)
    lat_x = local_lattice[0].astype(jnp.float32)
    lat_y = local_lattice[1].astype(jnp.float32)
    local_count = positions.shape[1]
    block_rows = min(384, local_count)
    block_count = local_count // block_rows
    pos_x = positions[0].reshape(block_count, block_rows)
    pos_y = positions[1].reshape(block_count, block_rows)
    partial_value = lax.map(
        lambda coords: orbital_block(coords[0], coords[1], lat_x, lat_y, right_cos, right_sin),
        (pos_x, pos_y),
    )
    partial_value = partial_value.reshape(local_count, right_cos.shape[1])
    walkers = float(walk_count * local_count // E)
    orbitals = lax.psum(partial_value, "band")
    gradient = fit_gradient(orbitals, spin_labels, features, orbital_head, walkers)
    return lax.psum(gradient, "walk")


def solution(mesh):
    return jax.shard_map(
        local,
        mesh=mesh,
        in_specs=(
            P(None, "walk"),
            P(None, "walk", "band"),
            P(),
            P("walk"),
            P(),
            P("walk", None),
            P(),
        ),
        out_specs=P(),
        check_vma=False,
    )
```

profile of v0, /device:TPU:0, one launch (start us, length us, event | category | flops | bytes accessed | tf_op | source)
XLA Modules:
  0.0 891.4 jit_solution(2126646476932792642)
XLA Ops:
  6.5 6.1 copy.31
  12.7 79.9 %all-gather.2.cloned.1.call-done = bf16[2,18432,128]{2,0,1:T(2,128)(2,1)} async-done(((bf16[2,1152,128]{2,0,1:T(2,128)(2,1)}), bf16[2,18432,128]{2,0,1:T(2,128)(2,1)}) %all-gather.2.cloned.1.call-update) | async-done | bytes 9437200 | tf_op jit(solution)/shard_map/all_gather | solution.py:67
  92.5 5.0 all-to-all-start
  97.9 0.9 fusion.32
  98.9 105.0 %all-to-all-done = bf16[2,18432,128]{2,0,1:T(2,128)(2,1)} async-done(((bf16[2,18432,128]{2,0,1:T(2,128)(2,1)}), bf16[2,18432,128]{2,0,1:T(2,128)(2,1)}, u32[]{:S(2)}, u32[]{:S(2)}) %all-to-all-start) | async-done | bytes 9437216 | tf_op jit(solution)/shard_map/all_to_all | solution.py:68
  203.9 10.1 %copy.32 = bf16[2,18432,128]{2,1,0:T(8,128)(2,1)} copy(bf16[2,18432,128]{2,0,1:T(2,128)(2,1)} %all-to-all-done) | data formatting | bytes 18874368 | tf_op jit(solution)/shard_map/all_to_all | solution.py:68
  214.0 12.9 %copy.33 = bf16[2,2304,8,128]{1,3,2,0:T(8,128)(2,1)} copy(bf16[2,2304,8,128]{3,1,2,0:T(8,128)(2,1)} %bitcast.33) | data formatting | bytes 18874368 | tf_op jit(solution)/shard_map/all_to_all | solution.py:68
  226.9 18.4 %copy.34 = bf16[2,2304,1024]{1,0,2:T(2,128)(2,1)} copy(bf16[2,2304,1024]{1,2,0:T(8,128)(2,1)} %bitcast.34) | data formatting | bytes 18874368 | tf_op jit(solution)/shard_map/all_to_all | solution.py:68
  245.3 6.1 gather_fusion
  251.4 0.8 fusion.31
  252.2 1.2 fusion.37
  253.6 1.5 maximum_convert_fusion.1
  255.0 3.0 copy.35
  258.0 1.9 copy.36
  259.9 364.3 %while.10 = (s32[]{:T(128)}, f32[8,384,192]{1,0,2:T(8,128)}, f32[8,384]{1,0:T(8,128)S(1)}, f32[2304]{0:T(1024)S(1)}, f32[8,384]{1,0:T(8,128)S(1)}, /*index=5*/f3...) while((s32[]{:T(128)}, f32[8,384,192]{1,0,2:T(8,128)}, ...), condition=%wide.region_1.2_spmd, body=%wide.region_0.1_spmd.sunk | while | flops 4084015104 | bytes 12730505 | solution.py:82
  282.6 18.3 %fusion.54 = f32[384,192]{0,1:T(8,128)S(1)} fusion(f32[2304,192]{1,0:T(8,128)} %get-tuple-element.200, f32[2304]{0:T(1024)S(1)} %get-tuple-element.198, f32[384]{0:T(512)S(1)} %get-tuple-element.171, f32[2304]{0:T(1024)S(1)} %get-tuple-element.196, f32[384]{0:T(512)S(1)} %get-tuple-element.172), kind=kOutput, calls=%fused_computation.1.clone.1 | convolution fusion | flops 2041970688 | bytes 2085888 | tf_op jit(solution)/shard_map/while/body/eval_jaxpr/dot_general | solution.py:17
  300.9 16.4 %fusion.55 = f32[1,384,192]{1,2,0:T(8,128)S(1)} fusion(f32[384,192]{0,1:T(8,128)S(1)} %fusion.54, f32[2304,192]{1,0:T(8,128)S(1)} %copy-done.2, f32[2304]{0:T(1024)S(1)} %get-tuple-element.198, f32[384]{0:T(512)S(1)} %get-tuple-element.171, f32[2304]{0:T(1024)S(1)} %get-tuple-element.196, f32[384]{0:T(512)S(1)} %get-tuple-element.172), kind=kOutput, calls=%fused_computation.17.clone.1 | convolution fusion | flops 2042044416 | bytes 2380800 | tf_op jit(solution)/shard_map/while/body/eval_jaxpr/dot_general | solution.py:14
  317.7 7.3 dynamic_update_slice.5
  325.0 18.3 %fusion.54 = f32[384,192]{0,1:T(8,128)S(1)} fusion(f32[2304,192]{1,0:T(8,128)} %get-tuple-element.200, f32[2304]{0:T(1024)S(1)} %get-tuple-element.198, f32[384]{0:T(512)S(1)} %get-tuple-element.171, f32[2304]{0:T(1024)S(1)} %get-tuple-element.196, f32[384]{0:T(512)S(1)} %get-tuple-element.172), kind=kOutput, calls=%fused_computation.1.clone.1 | convolution fusion | flops 2041970688 | bytes 2085888 | tf_op jit(solution)/shard_map/while/body/eval_jaxpr/dot_general | solution.py:17
  343.3 16.4 %fusion.55 = f32[1,384,192]{1,2,0:T(8,128)S(1)} fusion(f32[384,192]{0,1:T(8,128)S(1)} %fusion.54, f32[2304,192]{1,0:T(8,128)S(1)} %copy-done.2, f32[2304]{0:T(1024)S(1)} %get-tuple-element.198, f32[384]{0:T(512)S(1)} %get-tuple-element.171, f32[2304]{0:T(1024)S(1)} %get-tuple-element.196, f32[384]{0:T(512)S(1)} %get-tuple-element.172), kind=kOutput, calls=%fused_computation.17.clone.1 | convolution fusion | flops 2042044416 | bytes 2380800 | tf_op jit(solution)/shard_map/while/body/eval_jaxpr/dot_general | solution.py:14
  360.0 7.3 dynamic_update_slice.5
  367.4 18.3 %fusion.54 = f32[384,192]{0,1:T(8,128)S(1)} fusion(f32[2304,192]{1,0:T(8,128)} %get-tuple-element.200, f32[2304]{0:T(1024)S(1)} %get-tuple-element.198, f32[384]{0:T(512)S(1)} %get-tuple-element.171, f32[2304]{0:T(1024)S(1)} %get-tuple-element.196, f32[384]{0:T(512)S(1)} %get-tuple-element.172), kind=kOutput, calls=%fused_computation.1.clone.1 | convolution fusion | flops 2041970688 | bytes 2085888 | tf_op jit(solution)/shard_map/while/body/eval_jaxpr/dot_general | solution.py:17
  385.7 16.4 %fusion.55 = f32[1,384,192]{1,2,0:T(8,128)S(1)} fusion(f32[384,192]{0,1:T(8,128)S(1)} %fusion.54, f32[2304,192]{1,0:T(8,128)S(1)} %copy-done.2, f32[2304]{0:T(1024)S(1)} %get-tuple-element.198, f32[384]{0:T(512)S(1)} %get-tuple-element.171, f32[2304]{0:T(1024)S(1)} %get-tuple-element.196, f32[384]{0:T(512)S(1)} %get-tuple-element.172), kind=kOutput, calls=%fused_computation.17.clone.1 | convolution fusion | flops 2042044416 | bytes 2380800 | tf_op jit(solution)/shard_map/while/body/eval_jaxpr/dot_general | solution.py:14
  402.4 7.3 dynamic_update_slice.5
  409.7 18.3 %fusion.54 = f32[384,192]{0,1:T(8,128)S(1)} fusion(f32[2304,192]{1,0:T(8,128)} %get-tuple-element.200, f32[2304]{0:T(1024)S(1)} %get-tuple-element.198, f32[384]{0:T(512)S(1)} %get-tuple-element.171, f32[2304]{0:T(1024)S(1)} %get-tuple-element.196, f32[384]{0:T(512)S(1)} %get-tuple-element.172), kind=kOutput, calls=%fused_computation.1.clone.1 | convolution fusion | flops 2041970688 | bytes 2085888 | tf_op jit(solution)/shard_map/while/body/eval_jaxpr/dot_general | solution.py:17
  428.1 16.4 %fusion.55 = f32[1,384,192]{1,2,0:T(8,128)S(1)} fusion(f32[384,192]{0,1:T(8,128)S(1)} %fusion.54, f32[2304,192]{1,0:T(8,128)S(1)} %copy-done.2, f32[2304]{0:T(1024)S(1)} %get-tuple-element.198, f32[384]{0:T(512)S(1)} %get-tuple-element.171, f32[2304]{0:T(1024)S(1)} %get-tuple-element.196, f32[384]{0:T(512)S(1)} %get-tuple-element.172), kind=kOutput, calls=%fused_computation.17.clone.1 | convolution fusion | flops 2042044416 | bytes 2380800 | tf_op jit(solution)/shard_map/while/body/eval_jaxpr/dot_general | solution.py:14
  444.8 7.3 dynamic_update_slice.5
  452.1 18.3 %fusion.54 = f32[384,192]{0,1:T(8,128)S(1)} fusion(f32[2304,192]{1,0:T(8,128)} %get-tuple-element.200, f32[2304]{0:T(1024)S(1)} %get-tuple-element.198, f32[384]{0:T(512)S(1)} %get-tuple-element.171, f32[2304]{0:T(1024)S(1)} %get-tuple-element.196, f32[384]{0:T(512)S(1)} %get-tuple-element.172), kind=kOutput, calls=%fused_computation.1.clone.1 | convolution fusion | flops 2041970688 | bytes 2085888 | tf_op jit(solution)/shard_map/while/body/eval_jaxpr/dot_general | solution.py:17
  470.4 16.4 %fusion.55 = f32[1,384,192]{1,2,0:T(8,128)S(1)} fusion(f32[384,192]{0,1:T(8,128)S(1)} %fusion.54, f32[2304,192]{1,0:T(8,128)S(1)} %copy-done.2, f32[2304]{0:T(1024)S(1)} %get-tuple-element.198, f32[384]{0:T(512)S(1)} %get-tuple-element.171, f32[2304]{0:T(1024)S(1)} %get-tuple-element.196, f32[384]{0:T(512)S(1)} %get-tuple-element.172), kind=kOutput, calls=%fused_computation.17.clone.1 | convolution fusion | flops 2042044416 | bytes 2380800 | tf_op jit(solution)/shard_map/while/body/eval_jaxpr/dot_general | solution.py:14
  487.2 7.3 dynamic_update_slice.5
  494.5 18.3 %fusion.54 = f32[384,192]{0,1:T(8,128)S(1)} fusion(f32[2304,192]{1,0:T(8,128)} %get-tuple-element.200, f32[2304]{0:T(1024)S(1)} %get-tuple-element.198, f32[384]{0:T(512)S(1)} %get-tuple-element.171, f32[2304]{0:T(1024)S(1)} %get-tuple-element.196, f32[384]{0:T(512)S(1)} %get-tuple-element.172), kind=kOutput, calls=%fused_computation.1.clone.1 | convolution fusion | flops 2041970688 | bytes 2085888 | tf_op jit(solution)/shard_map/while/body/eval_jaxpr/dot_general | solution.py:17
  512.8 16.4 %fusion.55 = f32[1,384,192]{1,2,0:T(8,128)S(1)} fusion(f32[384,192]{0,1:T(8,128)S(1)} %fusion.54, f32[2304,192]{1,0:T(8,128)S(1)} %copy-done.2, f32[2304]{0:T(1024)S(1)} %get-tuple-element.198, f32[384]{0:T(512)S(1)} %get-tuple-element.171, f32[2304]{0:T(1024)S(1)} %get-tuple-element.196, f32[384]{0:T(512)S(1)} %get-tuple-element.172), kind=kOutput, calls=%fused_computation.17.clone.1 | convolution fusion | flops 2042044416 | bytes 2380800 | tf_op jit(solution)/shard_map/while/body/eval_jaxpr/dot_general | solution.py:14
  529.5 7.3 dynamic_update_slice.5
  536.9 18.3 %fusion.54 = f32[384,192]{0,1:T(8,128)S(1)} fusion(f32[2304,192]{1,0:T(8,128)} %get-tuple-element.200, f32[2304]{0:T(1024)S(1)} %get-tuple-element.198, f32[384]{0:T(512)S(1)} %get-tuple-element.171, f32[2304]{0:T(1024)S(1)} %get-tuple-element.196, f32[384]{0:T(512)S(1)} %get-tuple-element.172), kind=kOutput, calls=%fused_computation.1.clone.1 | convolution fusion | flops 2041970688 | bytes 2085888 | tf_op jit(solution)/shard_map/while/body/eval_jaxpr/dot_general | solution.py:17
  555.2 16.4 %fusion.55 = f32[1,384,192]{1,2,0:T(8,128)S(1)} fusion(f32[384,192]{0,1:T(8,128)S(1)} %fusion.54, f32[2304,192]{1,0:T(8,128)S(1)} %copy-done.2, f32[2304]{0:T(1024)S(1)} %get-tuple-element.198, f32[384]{0:T(512)S(1)} %get-tuple-element.171, f32[2304]{0:T(1024)S(1)} %get-tuple-element.196, f32[384]{0:T(512)S(1)} %get-tuple-element.172), kind=kOutput, calls=%fused_computation.17.clone.1 | convolution fusion | flops 2042044416 | bytes 2380800 | tf_op jit(solution)/shard_map/while/body/eval_jaxpr/dot_general | solution.py:14
  571.9 7.3 dynamic_update_slice.5
  579.2 18.3 %fusion.54 = f32[384,192]{0,1:T(8,128)S(1)} fusion(f32[2304,192]{1,0:T(8,128)} %get-tuple-element.200, f32[2304]{0:T(1024)S(1)} %get-tuple-element.198, f32[384]{0:T(512)S(1)} %get-tuple-element.171, f32[2304]{0:T(1024)S(1)} %get-tuple-element.196, f32[384]{0:T(512)S(1)} %get-tuple-element.172), kind=kOutput, calls=%fused_computation.1.clone.1 | convolution fusion | flops 2041970688 | bytes 2085888 | tf_op jit(solution)/shard_map/while/body/eval_jaxpr/dot_general | solution.py:17
  597.6 16.4 %fusion.55 = f32[1,384,192]{1,2,0:T(8,128)S(1)} fusion(f32[384,192]{0,1:T(8,128)S(1)} %fusion.54, f32[2304,192]{1,0:T(8,128)S(1)} %copy-done.2, f32[2304]{0:T(1024)S(1)} %get-tuple-element.198, f32[384]{0:T(512)S(1)} %get-tuple-element.171, f32[2304]{0:T(1024)S(1)} %get-tuple-element.196, f32[384]{0:T(512)S(1)} %get-tuple-element.172), kind=kOutput, calls=%fused_computation.17.clone.1 | convolution fusion | flops 2042044416 | bytes 2380800 | tf_op jit(solution)/shard_map/while/body/eval_jaxpr/dot_general | solution.py:14
  614.3 7.3 dynamic_update_slice.5
  624.2 3.5 copy.42
  627.8 0.6 copy-done.5
  628.6 2.1 fusion.38
  630.7 114.0 %all-reduce.3.cloned.1.call-done = f32[3072,192]{0,1:T(8,128)} async-done(((f32[3072,192]{0,1:T(8,128)}), f32[3072,192]{0,1:T(8,128)}) %all-reduce.3.cloned.1.call-update) | async-done | bytes 2359312 | tf_op jit(solution)/shard_map/psum | solution.py:88
  744.7 1.9 slice_select_fusion.2
  746.6 0.5 copy-done.1
  747.5 1.9 fusion.28
  749.4 133.6 %all-reduce.5.cloned.1.call-done = f32[256,192]{0,1:T(8,128)} async-done(((f32[256,192]{0,1:T(8,128)}), f32[256,192]{0,1:T(8,128)}) %all-reduce.5.cloned.1.call-update) | async-done | bytes 196624 | tf_op jit(solution)/shard_map/psum | solution.py:90
  883.0 1.6 copy.58
  (61 shorter events, 3.8 us)
Async XLA Ops:
  6.5 621.9 %copy-start = (bf16[3072,256]{1,0:T(8,128)(2,1)S(1)}, bf16[3072,256]{1,0:T(8,128)(2,1)}, u32[]{:S(2)}) copy-start(bf16[3072,256]{1,0:T(8,128)(2,1)} %param.14) | copy-start | bytes 4718596
  6.5 86.0 %all-gather.2.cloned.1.call-start = ((), (), s32[]{:S(2)}) async-start(), calls=%async_computation.1 | async-start | bytes 10027008 | tf_op jit(solution)/shard_map/all_gather | solution.py:67
  12.6 85.0 %copy-start.6 = (s32[2,48]{1,0:T(2,128)S(1)}, s32[2,48]{1,0:T(2,128)}, u32[]{:S(2)}) copy-start(s32[2,48]{1,0:T(2,128)} %param.13) | copy-start | bytes 1156
  12.6 85.2 %copy-start.4 = (f32[2,3072]{1,0:T(2,128)S(1)}, f32[2,3072]{1,0:T(2,128)}, u32[]{:S(2)}) copy-start(f32[2,3072]{1,0:T(2,128)} %param.9) | copy-start | bytes 73732
  92.5 111.3 %all-to-all-start = ((bf16[2,18432,128]{2,0,1:T(2,128)(2,1)}), bf16[2,18432,128]{2,0,1:T(2,128)(2,1)}, u32[]{:S(2)}, u32[]{:S(2)}) async-start(bf16[2,18432,128]{2,0,1:T(2,128)(2,1)} %all-gather.2.cloned.1.call-done), calls=%async_computation | async-start | bytes 18874368 | tf_op jit(solution)/shard_map/all_to_all | solution.py:68
  97.6 647.1 %all-reduce.3.cloned.1.call-start = ((), (), s32[]{:S(2)}) async-start(), calls=%async_computation.2 | async-start | bytes 4718592 | tf_op jit(solution)/shard_map/psum | solution.py:88
  282.6 18.3 %copy-start.2 = (f32[2304,192]{1,0:T(8,128)S(1)}, f32[2304,192]{1,0:T(8,128)}, u32[]{:S(2)}) copy-start(f32[2304,192]{1,0:T(8,128)} %get-tuple-element.199) | copy-start | bytes 5308420 | tf_op jit(solution)/shard_map/while
  325.0 18.3 %copy-start.2 = (f32[2304,192]{1,0:T(8,128)S(1)}, f32[2304,192]{1,0:T(8,128)}, u32[]{:S(2)}) copy-start(f32[2304,192]{1,0:T(8,128)} %get-tuple-element.199) | copy-start | bytes 5308420 | tf_op jit(solution)/shard_map/while
  367.3 18.3 %copy-start.2 = (f32[2304,192]{1,0:T(8,128)S(1)}, f32[2304,192]{1,0:T(8,128)}, u32[]{:S(2)}) copy-start(f32[2304,192]{1,0:T(8,128)} %get-tuple-element.199) | copy-start | bytes 5308420 | tf_op jit(solution)/shard_map/while
  409.7 18.3 %copy-start.2 = (f32[2304,192]{1,0:T(8,128)S(1)}, f32[2304,192]{1,0:T(8,128)}, u32[]{:S(2)}) copy-start(f32[2304,192]{1,0:T(8,128)} %get-tuple-element.199) | copy-start | bytes 5308420 | tf_op jit(solution)/shard_map/while
  452.1 18.3 %copy-start.2 = (f32[2304,192]{1,0:T(8,128)S(1)}, f32[2304,192]{1,0:T(8,128)}, u32[]{:S(2)}) copy-start(f32[2304,192]{1,0:T(8,128)} %get-tuple-element.199) | copy-start | bytes 5308420 | tf_op jit(solution)/shard_map/while
  494.5 18.3 %copy-start.2 = (f32[2304,192]{1,0:T(8,128)S(1)}, f32[2304,192]{1,0:T(8,128)}, u32[]{:S(2)}) copy-start(f32[2304,192]{1,0:T(8,128)} %get-tuple-element.199) | copy-start | bytes 5308420 | tf_op jit(solution)/shard_map/while
  536.8 18.3 %copy-start.2 = (f32[2304,192]{1,0:T(8,128)S(1)}, f32[2304,192]{1,0:T(8,128)}, u32[]{:S(2)}) copy-start(f32[2304,192]{1,0:T(8,128)} %get-tuple-element.199) | copy-start | bytes 5308420 | tf_op jit(solution)/shard_map/while
  579.2 18.3 %copy-start.2 = (f32[2304,192]{1,0:T(8,128)S(1)}, f32[2304,192]{1,0:T(8,128)}, u32[]{:S(2)}) copy-start(f32[2304,192]{1,0:T(8,128)} %get-tuple-element.199) | copy-start | bytes 5308420 | tf_op jit(solution)/shard_map/while
  627.7 0.7 copy-start.5
  627.7 0.9 copy-start.3
  627.8 255.3 %all-reduce.5.cloned.1.call-start = ((), (), s32[]{:S(2)}) async-start(), calls=%async_computation.3 | async-start | bytes 393216 | tf_op jit(solution)/shard_map/psum | solution.py:90
  744.7 2.4 copy-start.1
Sparse Core Ops, SparseCore 0:
  12.7 79.7 all-gather.1
  627.9 116.7 all-reduce.2
  749.6 133.4 all-reduce.4
where the time goes:
time: 901 us; the launch traced here: 891 us
  waiting for transfers between devices  433 us (48%)
  matrix products  282 us (31%)
  local copies, waits for them, and re-layouts  127 us (14%)
  loops' own time  25.6 us (3%)
  between operations  13.4 us (1%)
    dot_general x8, matrix products, orbital_block(): jnp.dot(sine_part, right_sin, precision=lax.Precision.HIGHEST, preferred_...  146 us
    psum x1, waiting for transfers between devices, local(): return lax.psum(gradient, 'walk')  134 us
    dot_general x8, matrix products, orbital_block(): jnp.dot(cosine, right_cos, precision=lax.Precision.HIGHEST, preferred_ele...  131 us
    psum x1, waiting for transfers between devices, local(): orbitals = lax.psum(partial_value, 'band')  114 us
    all_to_all x1, waiting for transfers between devices, local(): lax.all_to_all(gathered, 'band', split_axis=1, concat_axis=2, tiled=True)  105 us
    all_gather x1, waiting for transfers between devices, local(): gathered = lax.all_gather(coefficients, 'walk', axis=1, tiled=True)  79.9 us
    dynamic_update_slice x16, local copies, waits for them, and re-layouts, local(): lax.map(lambda coords: orbital_block(coords[0], coords[1], lat_x, lat_y,...  60.7 us
    all_to_all x3, local copies, waits for them, and re-layouts, local(): lax.all_to_all(gathered, 'band', split_axis=1, concat_axis=2, tiled=True)  41.4 us
  transfers between devices with their start and end apart: 4, of which 4 were waited for; matrix products, arithmetic and copies ran while one was open for 0% of the time, Pallas kernels for 0%

commit v1 on v0

--- a/solution.py
+++ b/solution.py
@@ -85,7 +85,7 @@
     )
     partial_value = partial_value.reshape(local_count, right_cos.shape[1])
     walkers = float(walk_count * local_count // E)
-    orbitals = lax.psum(partial_value, "band")
+    orbitals = jnp.sum(lax.all_gather(partial_value, "band"), axis=0)
     gradient = fit_gradient(orbitals, spin_labels, features, orbital_head, walkers)
     return lax.psum(gradient, "walk")
 

time: 901 us -> 1020 us (1.13)
  waiting for transfers between devices: 433 us -> 538 us
    all_gather x0 -> x1, waiting for transfers between devices: none -> 220 us  [local(): orbitals = jnp.sum(lax.all_gather(partial_value, 'band'), axis=0)]
    psum x1 -> x0, waiting for transfers between devices: 114 us -> none  [local(): orbitals = lax.psum(partial_value, 'band')]
where the time goes in v1:
time: 1020 us; the launch traced here: 1010 us
  waiting for transfers between devices  538 us (53%)
  matrix products  282 us (28%)
  local copies, waits for them, and re-layouts  127 us (12%)
  loops' own time  26.9 us (3%)
  other arithmetic  15.6 us (2%)
  between operations  13.4 us (1%)
    all_gather x1, waiting for transfers between devices, local(): orbitals = jnp.sum(lax.all_gather(partial_value, 'band'), axis=0)  220 us
    dot_general x8, matrix products, orbital_block(): jnp.dot(sine_part, right_sin, precision=lax.Precision.HIGHEST, preferred_...  146 us
    psum x1, waiting for transfers between devices, local(): return lax.psum(gradient, 'walk')  133 us
    dot_general x8, matrix products, orbital_block(): jnp.dot(cosine, right_cos, precision=lax.Precision.HIGHEST, preferred_ele...  131 us
    all_to_all x1, waiting for transfers between devices, local(): lax.all_to_all(gathered, 'band', split_axis=1, concat_axis=2, tiled=True)  105 us
    all_gather x1, waiting for transfers between devices, local(): gathered = lax.all_gather(coefficients, 'walk', axis=1, tiled=True)  79.9 us
    dynamic_update_slice x16, local copies, waits for them, and re-layouts, local(): lax.map(lambda coords: orbital_block(coords[0], coords[1], lat_x, lat_y,...  60.7 us
    all_to_all x3, local copies, waits for them, and re-layouts, local(): lax.all_to_all(gathered, 'band', split_axis=1, concat_axis=2, tiled=True)  41.4 us
  transfers between devices with their start and end apart: 4, of which 4 were waited for; matrix products, arithmetic and copies ran while one was open for 0% of the time, Pallas kernels for 0%

profile of v1, /device:TPU:0, one launch (start us, length us, event | category | flops | bytes accessed | tf_op | source)
XLA Modules:
  0.0 1008.0 jit_solution(3903076307778801097)
XLA Ops:
  6.5 6.1 copy.30
  12.7 79.9 %all-gather.3.cloned.1.call-done = bf16[2,18432,128]{2,0,1:T(2,128)(2,1)} async-done(((bf16[2,1152,128]{2,0,1:T(2,128)(2,1)}), bf16[2,18432,128]{2,0,1:T(2,128)(2,1)}) %all-gather.3.cloned.1.call-update) | async-done | bytes 9437200 | tf_op jit(solution)/shard_map/all_gather | solution.py:67
  92.5 5.0 all-to-all-start
  97.9 0.9 fusion.32
  98.9 105.0 %all-to-all-done = bf16[2,18432,128]{2,0,1:T(2,128)(2,1)} async-done(((bf16[2,18432,128]{2,0,1:T(2,128)(2,1)}), bf16[2,18432,128]{2,0,1:T(2,128)(2,1)}, u32[]{:S(2)}, u32[]{:S(2)}) %all-to-all-start) | async-done | bytes 9437216 | tf_op jit(solution)/shard_map/all_to_all | solution.py:68
  203.9 10.1 %copy.31 = bf16[2,18432,128]{2,1,0:T(8,128)(2,1)} copy(bf16[2,18432,128]{2,0,1:T(2,128)(2,1)} %all-to-all-done) | data formatting | bytes 18874368 | tf_op jit(solution)/shard_map/all_to_all | solution.py:68
  214.0 12.9 %copy.32 = bf16[2,2304,8,128]{1,3,2,0:T(8,128)(2,1)} copy(bf16[2,2304,8,128]{3,1,2,0:T(8,128)(2,1)} %bitcast.31) | data formatting | bytes 18874368 | tf_op jit(solution)/shard_map/all_to_all | solution.py:68
  226.9 18.4 %copy.33 = bf16[2,2304,1024]{1,0,2:T(2,128)(2,1)} copy(bf16[2,2304,1024]{1,2,0:T(8,128)(2,1)} %bitcast.32) | data formatting | bytes 18874368 | tf_op jit(solution)/shard_map/all_to_all | solution.py:68
  245.3 6.1 gather_fusion
  251.4 0.8 fusion.31
  252.2 1.2 fusion.37
  253.6 1.5 maximum_convert_fusion.1
  255.0 3.0 copy.34
  258.0 1.9 copy.35
  259.9 365.6 %while.10 = (s32[]{:T(128)}, f32[8,384,192]{1,0,2:T(8,128)}, f32[8,384]{1,0:T(8,128)S(1)}, f32[2304]{0:T(1024)S(1)}, f32[8,384]{1,0:T(8,128)S(1)}, /*index=5*/f3...) while((s32[]{:T(128)}, f32[8,384,192]{1,0,2:T(8,128)}, ...), condition=%wide.region_1.2_spmd, body=%wide.region_0.1_spmd.sunk | while | flops 4084015104 | bytes 12730505 | solution.py:82
  282.6 18.3 %fusion.54 = f32[384,192]{0,1:T(8,128)S(1)} fusion(f32[2304,192]{1,0:T(8,128)} %get-tuple-element.200, f32[2304]{0:T(1024)S(1)} %get-tuple-element.198, f32[384]{0:T(512)S(1)} %get-tuple-element.171, f32[2304]{0:T(1024)S(1)} %get-tuple-element.196, f32[384]{0:T(512)S(1)} %get-tuple-element.172), kind=kOutput, calls=%fused_computation.1.clone.1 | convolution fusion | flops 2041970688 | bytes 2085888 | tf_op jit(solution)/shard_map/while/body/eval_jaxpr/dot_general | solution.py:17
  300.9 16.4 %fusion.55 = f32[1,384,192]{1,2,0:T(8,128)S(1)} fusion(f32[384,192]{0,1:T(8,128)S(1)} %fusion.54, f32[2304,192]{1,0:T(8,128)S(1)} %copy-done.2, f32[2304]{0:T(1024)S(1)} %get-tuple-element.198, f32[384]{0:T(512)S(1)} %get-tuple-element.171, f32[2304]{0:T(1024)S(1)} %get-tuple-element.196, f32[384]{0:T(512)S(1)} %get-tuple-element.172), kind=kOutput, calls=%fused_computation.17.clone.1 | convolution fusion | flops 2042044416 | bytes 2380800 | tf_op jit(solution)/shard_map/while/body/eval_jaxpr/dot_general | solution.py:14
  317.7 7.3 dynamic_update_slice.5
  325.0 18.3 %fusion.54 = f32[384,192]{0,1:T(8,128)S(1)} fusion(f32[2304,192]{1,0:T(8,128)} %get-tuple-element.200, f32[2304]{0:T(1024)S(1)} %get-tuple-element.198, f32[384]{0:T(512)S(1)} %get-tuple-element.171, f32[2304]{0:T(1024)S(1)} %get-tuple-element.196, f32[384]{0:T(512)S(1)} %get-tuple-element.172), kind=kOutput, calls=%fused_computation.1.clone.1 | convolution fusion | flops 2041970688 | bytes 2085888 | tf_op jit(solution)/shard_map/while/body/eval_jaxpr/dot_general | solution.py:17
  343.3 16.4 %fusion.55 = f32[1,384,192]{1,2,0:T(8,128)S(1)} fusion(f32[384,192]{0,1:T(8,128)S(1)} %fusion.54, f32[2304,192]{1,0:T(8,128)S(1)} %copy-done.2, f32[2304]{0:T(1024)S(1)} %get-tuple-element.198, f32[384]{0:T(512)S(1)} %get-tuple-element.171, f32[2304]{0:T(1024)S(1)} %get-tuple-element.196, f32[384]{0:T(512)S(1)} %get-tuple-element.172), kind=kOutput, calls=%fused_computation.17.clone.1 | convolution fusion | flops 2042044416 | bytes 2380800 | tf_op jit(solution)/shard_map/while/body/eval_jaxpr/dot_general | solution.py:14
  360.0 7.3 dynamic_update_slice.5
  367.4 18.3 %fusion.54 = f32[384,192]{0,1:T(8,128)S(1)} fusion(f32[2304,192]{1,0:T(8,128)} %get-tuple-element.200, f32[2304]{0:T(1024)S(1)} %get-tuple-element.198, f32[384]{0:T(512)S(1)} %get-tuple-element.171, f32[2304]{0:T(1024)S(1)} %get-tuple-element.196, f32[384]{0:T(512)S(1)} %get-tuple-element.172), kind=kOutput, calls=%fused_computation.1.clone.1 | convolution fusion | flops 2041970688 | bytes 2085888 | tf_op jit(solution)/shard_map/while/body/eval_jaxpr/dot_general | solution.py:17
  385.7 16.4 %fusion.55 = f32[1,384,192]{1,2,0:T(8,128)S(1)} fusion(f32[384,192]{0,1:T(8,128)S(1)} %fusion.54, f32[2304,192]{1,0:T(8,128)S(1)} %copy-done.2, f32[2304]{0:T(1024)S(1)} %get-tuple-element.198, f32[384]{0:T(512)S(1)} %get-tuple-element.171, f32[2304]{0:T(1024)S(1)} %get-tuple-element.196, f32[384]{0:T(512)S(1)} %get-tuple-element.172), kind=kOutput, calls=%fused_computation.17.clone.1 | convolution fusion | flops 2042044416 | bytes 2380800 | tf_op jit(solution)/shard_map/while/body/eval_jaxpr/dot_general | solution.py:14
  402.4 7.3 dynamic_update_slice.5
  409.7 18.3 %fusion.54 = f32[384,192]{0,1:T(8,128)S(1)} fusion(f32[2304,192]{1,0:T(8,128)} %get-tuple-element.200, f32[2304]{0:T(1024)S(1)} %get-tuple-element.198, f32[384]{0:T(512)S(1)} %get-tuple-element.171, f32[2304]{0:T(1024)S(1)} %get-tuple-element.196, f32[384]{0:T(512)S(1)} %get-tuple-element.172), kind=kOutput, calls=%fused_computation.1.clone.1 | convolution fusion | flops 2041970688 | bytes 2085888 | tf_op jit(solution)/shard_map/while/body/eval_jaxpr/dot_general | solution.py:17
  428.1 16.4 %fusion.55 = f32[1,384,192]{1,2,0:T(8,128)S(1)} fusion(f32[384,192]{0,1:T(8,128)S(1)} %fusion.54, f32[2304,192]{1,0:T(8,128)S(1)} %copy-done.2, f32[2304]{0:T(1024)S(1)} %get-tuple-element.198, f32[384]{0:T(512)S(1)} %get-tuple-element.171, f32[2304]{0:T(1024)S(1)} %get-tuple-element.196, f32[384]{0:T(512)S(1)} %get-tuple-element.172), kind=kOutput, calls=%fused_computation.17.clone.1 | convolution fusion | flops 2042044416 | bytes 2380800 | tf_op jit(solution)/shard_map/while/body/eval_jaxpr/dot_general | solution.py:14
  444.8 7.3 dynamic_update_slice.5
  452.1 18.3 %fusion.54 = f32[384,192]{0,1:T(8,128)S(1)} fusion(f32[2304,192]{1,0:T(8,128)} %get-tuple-element.200, f32[2304]{0:T(1024)S(1)} %get-tuple-element.198, f32[384]{0:T(512)S(1)} %get-tuple-element.171, f32[2304]{0:T(1024)S(1)} %get-tuple-element.196, f32[384]{0:T(512)S(1)} %get-tuple-element.172), kind=kOutput, calls=%fused_computation.1.clone.1 | convolution fusion | flops 2041970688 | bytes 2085888 | tf_op jit(solution)/shard_map/while/body/eval_jaxpr/dot_general | solution.py:17
  470.4 16.4 %fusion.55 = f32[1,384,192]{1,2,0:T(8,128)S(1)} fusion(f32[384,192]{0,1:T(8,128)S(1)} %fusion.54, f32[2304,192]{1,0:T(8,128)S(1)} %copy-done.2, f32[2304]{0:T(1024)S(1)} %get-tuple-element.198, f32[384]{0:T(512)S(1)} %get-tuple-element.171, f32[2304]{0:T(1024)S(1)} %get-tuple-element.196, f32[384]{0:T(512)S(1)} %get-tuple-element.172), kind=kOutput, calls=%fused_computation.17.clone.1 | convolution fusion | flops 2042044416 | bytes 2380800 | tf_op jit(solution)/shard_map/while/body/eval_jaxpr/dot_general | solution.py:14
  487.2 7.3 dynamic_update_slice.5
  494.5 18.3 %fusion.54 = f32[384,192]{0,1:T(8,128)S(1)} fusion(f32[2304,192]{1,0:T(8,128)} %get-tuple-element.200, f32[2304]{0:T(1024)S(1)} %get-tuple-element.198, f32[384]{0:T(512)S(1)} %get-tuple-element.171, f32[2304]{0:T(1024)S(1)} %get-tuple-element.196, f32[384]{0:T(512)S(1)} %get-tuple-element.172), kind=kOutput, calls=%fused_computation.1.clone.1 | convolution fusion | flops 2041970688 | bytes 2085888 | tf_op jit(solution)/shard_map/while/body/eval_jaxpr/dot_general | solution.py:17
  512.8 16.4 %fusion.55 = f32[1,384,192]{1,2,0:T(8,128)S(1)} fusion(f32[384,192]{0,1:T(8,128)S(1)} %fusion.54, f32[2304,192]{1,0:T(8,128)S(1)} %copy-done.2, f32[2304]{0:T(1024)S(1)} %get-tuple-element.198, f32[384]{0:T(512)S(1)} %get-tuple-element.171, f32[2304]{0:T(1024)S(1)} %get-tuple-element.196, f32[384]{0:T(512)S(1)} %get-tuple-element.172), kind=kOutput, calls=%fused_computation.17.clone.1 | convolution fusion | flops 2042044416 | bytes 2380800 | tf_op jit(solution)/shard_map/while/body/eval_jaxpr/dot_general | solution.py:14
  529.5 7.3 dynamic_update_slice.5
  536.9 18.3 %fusion.54 = f32[384,192]{0,1:T(8,128)S(1)} fusion(f32[2304,192]{1,0:T(8,128)} %get-tuple-element.200, f32[2304]{0:T(1024)S(1)} %get-tuple-element.198, f32[384]{0:T(512)S(1)} %get-tuple-element.171, f32[2304]{0:T(1024)S(1)} %get-tuple-element.196, f32[384]{0:T(512)S(1)} %get-tuple-element.172), kind=kOutput, calls=%fused_computation.1.clone.1 | convolution fusion | flops 2041970688 | bytes 2085888 | tf_op jit(solution)/shard_map/while/body/eval_jaxpr/dot_general | solution.py:17
  555.2 16.4 %fusion.55 = f32[1,384,192]{1,2,0:T(8,128)S(1)} fusion(f32[384,192]{0,1:T(8,128)S(1)} %fusion.54, f32[2304,192]{1,0:T(8,128)S(1)} %copy-done.2, f32[2304]{0:T(1024)S(1)} %get-tuple-element.198, f32[384]{0:T(512)S(1)} %get-tuple-element.171, f32[2304]{0:T(1024)S(1)} %get-tuple-element.196, f32[384]{0:T(512)S(1)} %get-tuple-element.172), kind=kOutput, calls=%fused_computation.17.clone.1 | convolution fusion | flops 2042044416 | bytes 2380800 | tf_op jit(solution)/shard_map/while/body/eval_jaxpr/dot_general | solution.py:14
  571.9 7.3 dynamic_update_slice.5
  579.2 18.3 %fusion.54 = f32[384,192]{0,1:T(8,128)S(1)} fusion(f32[2304,192]{1,0:T(8,128)} %get-tuple-element.200, f32[2304]{0:T(1024)S(1)} %get-tuple-element.198, f32[384]{0:T(512)S(1)} %get-tuple-element.171, f32[2304]{0:T(1024)S(1)} %get-tuple-element.196, f32[384]{0:T(512)S(1)} %get-tuple-element.172), kind=kOutput, calls=%fused_computation.1.clone.1 | convolution fusion | flops 2041970688 | bytes 2085888 | tf_op jit(solution)/shard_map/while/body/eval_jaxpr/dot_general | solution.py:17
  597.6 16.4 %fusion.55 = f32[1,384,192]{1,2,0:T(8,128)S(1)} fusion(f32[384,192]{0,1:T(8,128)S(1)} %fusion.54, f32[2304,192]{1,0:T(8,128)S(1)} %copy-done.2, f32[2304]{0:T(1024)S(1)} %get-tuple-element.198, f32[384]{0:T(512)S(1)} %get-tuple-element.171, f32[2304]{0:T(1024)S(1)} %get-tuple-element.196, f32[384]{0:T(512)S(1)} %get-tuple-element.172), kind=kOutput, calls=%fused_computation.17.clone.1 | convolution fusion | flops 2042044416 | bytes 2380800 | tf_op jit(solution)/shard_map/while/body/eval_jaxpr/dot_general | solution.py:14
  614.3 7.3 dynamic_update_slice.5
  625.6 3.2 all_gather_reshape.3
  628.9 0.6 copy-done.5
  629.7 2.1 fusion.38
  631.8 220.4 %all-gather.5.cloned.1.call-done = f32[8,3072,192]{1,2,0:T(8,128)} async-done(((f32[1,3072,192]{1,2,0:T(8,128)}), f32[8,3072,192]{1,2,0:T(8,128)}) %all-gather.5.cloned.1.call-update) | async-done | bytes 18874384 | tf_op jit(solution)/shard_map/all_gather | solution.py:88
  852.2 10.0 reduce_sum.9
  862.2 1.9 slice_select_fusion.2
  864.9 1.9 fusion.28
  866.9 132.7 %all-reduce.2.cloned.1.call-done = f32[256,192]{0,1:T(8,128)} async-done(((f32[256,192]{0,1:T(8,128)}), f32[256,192]{0,1:T(8,128)}) %all-reduce.2.cloned.1.call-update) | async-done | bytes 196624 | tf_op jit(solution)/shard_map/psum | solution.py:90
  999.6 1.6 copy.56
  (62 shorter events, 4.3 us)
Async XLA Ops:
  6.5 623.0 %copy-start = (bf16[3072,256]{1,0:T(8,128)(2,1)S(1)}, bf16[3072,256]{1,0:T(8,128)(2,1)}, u32[]{:S(2)}) copy-start(bf16[3072,256]{1,0:T(8,128)(2,1)} %param.14) | copy-start | bytes 4718596
  6.5 86.0 %all-gather.3.cloned.1.call-start = ((), (), s32[]{:S(2)}) async-start(), calls=%async_computation.1 | async-start | bytes 10027008 | tf_op jit(solution)/shard_map/all_gather | solution.py:67
  12.6 85.0 %copy-start.6 = (s32[2,48]{1,0:T(2,128)S(1)}, s32[2,48]{1,0:T(2,128)}, u32[]{:S(2)}) copy-start(s32[2,48]{1,0:T(2,128)} %param.13) | copy-start | bytes 1156
  12.6 85.2 %copy-start.4 = (f32[2,3072]{1,0:T(2,128)S(1)}, f32[2,3072]{1,0:T(2,128)}, u32[]{:S(2)}) copy-start(f32[2,3072]{1,0:T(2,128)} %param.9) | copy-start | bytes 73732
  92.5 111.3 %all-to-all-start = ((bf16[2,18432,128]{2,0,1:T(2,128)(2,1)}), bf16[2,18432,128]{2,0,1:T(2,128)(2,1)}, u32[]{:S(2)}, u32[]{:S(2)}) async-start(bf16[2,18432,128]{2,0,1:T(2,128)(2,1)} %all-gather.3.cloned.1.call-done), calls=%async_computation | async-start | bytes 18874368 | tf_op jit(solution)/shard_map/all_to_all | solution.py:68
  97.6 754.6 %all-gather.5.cloned.1.call-start = ((), (), s32[]{:S(2)}) async-start(), calls=%async_computation.2 | async-start | bytes 21233664 | tf_op jit(solution)/shard_map/all_gather | solution.py:88
  282.6 18.3 %copy-start.2 = (f32[2304,192]{1,0:T(8,128)S(1)}, f32[2304,192]{1,0:T(8,128)}, u32[]{:S(2)}) copy-start(f32[2304,192]{1,0:T(8,128)} %get-tuple-element.199) | copy-start | bytes 5308420 | tf_op jit(solution)/shard_map/while
  325.0 18.3 %copy-start.2 = (f32[2304,192]{1,0:T(8,128)S(1)}, f32[2304,192]{1,0:T(8,128)}, u32[]{:S(2)}) copy-start(f32[2304,192]{1,0:T(8,128)} %get-tuple-element.199) | copy-start | bytes 5308420 | tf_op jit(solution)/shard_map/while
  367.3 18.3 %copy-start.2 = (f32[2304,192]{1,0:T(8,128)S(1)}, f32[2304,192]{1,0:T(8,128)}, u32[]{:S(2)}) copy-start(f32[2304,192]{1,0:T(8,128)} %get-tuple-element.199) | copy-start | bytes 5308420 | tf_op jit(solution)/shard_map/while
  409.7 18.3 %copy-start.2 = (f32[2304,192]{1,0:T(8,128)S(1)}, f32[2304,192]{1,0:T(8,128)}, u32[]{:S(2)}) copy-start(f32[2304,192]{1,0:T(8,128)} %get-tuple-element.199) | copy-start | bytes 5308420 | tf_op jit(solution)/shard_map/while
  452.1 18.3 %copy-start.2 = (f32[2304,192]{1,0:T(8,128)S(1)}, f32[2304,192]{1,0:T(8,128)}, u32[]{:S(2)}) copy-start(f32[2304,192]{1,0:T(8,128)} %get-tuple-element.199) | copy-start | bytes 5308420 | tf_op jit(solution)/shard_map/while
  494.5 18.3 %copy-start.2 = (f32[2304,192]{1,0:T(8,128)S(1)}, f32[2304,192]{1,0:T(8,128)}, u32[]{:S(2)}) copy-start(f32[2304,192]{1,0:T(8,128)} %get-tuple-element.199) | copy-start | bytes 5308420 | tf_op jit(solution)/shard_map/while
  536.8 18.3 %copy-start.2 = (f32[2304,192]{1,0:T(8,128)S(1)}, f32[2304,192]{1,0:T(8,128)}, u32[]{:S(2)}) copy-start(f32[2304,192]{1,0:T(8,128)} %get-tuple-element.199) | copy-start | bytes 5308420 | tf_op jit(solution)/shard_map/while
  579.2 18.3 %copy-start.2 = (f32[2304,192]{1,0:T(8,128)S(1)}, f32[2304,192]{1,0:T(8,128)}, u32[]{:S(2)}) copy-start(f32[2304,192]{1,0:T(8,128)} %get-tuple-element.199) | copy-start | bytes 5308420 | tf_op jit(solution)/shard_map/while
  628.8 0.7 copy-start.5
  628.8 0.9 copy-start.3
  628.8 370.8 %all-reduce.2.cloned.1.call-start = ((), (), s32[]{:S(2)}) async-start(), calls=%async_computation.3 | async-start | bytes 393216 | tf_op jit(solution)/shard_map/psum | solution.py:90
  862.2 2.4 copy-start.1
Sparse Core Ops, SparseCore 0:
  12.7 79.7 all-gather.2
  628.9 223.1 all-gather.4
  867.0 132.5 all-reduce.1
